TPU v7x, 32 devices: a whole 2x2x4 slice. The times are simulated.
32 devices in a mesh: leaf: 8 (over z, y), rows: 4 (over x, core).
Axes of the slice: x: 2, y: 2, z: 4, core: 2. Of those that a mesh axis runs over, the one named last changes fastest.
Arguments:
- sigma_top: float32 [2048, 1024], P('leaf'), may hold values from -4 to 40, as said below
- panel_top: float32 [1024, 12288], P(None, 'leaf'), may hold values from -0.125 to 0.125
- diag_top: float32 [12288, 256], P('leaf'), may hold values from -4 to 20, as said below
- panel_mid: float32 [1024, 24576], P(None, ('leaf', 'rows')), may hold values from -0.125 to 0.125
- diag_mid: float32 [24576, 256], P(('leaf', 'rows')), may hold values from -4 to 20, as said below
- pattern_mid: int32 [4, 4], replicated, may hold values from 0 to 23, as said below
- panel_low: float32 [1024, 49152], P(None, ('leaf', 'rows')), may hold values from -0.125 to 0.125
- diag_low: float32 [49152, 256], P(('leaf', 'rows')), may hold values from -4 to 20, as said below
- pattern_low: int32 [8, 4], replicated, may hold values from 0 to 23, as said below
Outputs:
- cross_top: float32 [1024, 12288], P('rows', 'leaf')
- marginal_top: float32 [12288, 256], P(('leaf', 'rows'))
- cross_mid: float32 [1024, 24576], P(None, ('leaf', 'rows'))
- marginal_mid: float32 [24576, 256], P(('leaf', 'rows'))
- cross_low: float32 [1024, 49152], P(None, ('leaf', 'rows'))
- marginal_low: float32 [49152, 256], P(('leaf', 'rows'))
Inputs may be any that keep to these rules, and one draw needn't show every extreme that they name: Each block of 1024 rows of sigma_top is symmetric. `diag_top`: each 256 x 256 block is symmetric. `diag_mid`: each block of 256 rows is symmetric. `diag_low`: each block of 256 rows is symmetric. `pattern_mid`: the 4 entries of a row are different; rows 2i and 2i + 1 together name 8 different blocks. `pattern_low`: the 4 entries of a row are different; rows 2i and 2i + 1 together name 8 different blocks.
All inputs are finite; a program needn't handle non-finite values.
Results may differ from a plain program's by a relative error of at most 0.00009.
Values sent between devices are 32-bit elements; how exact they have to be, the bound alone decides.
A program may use at most 192 MiB of HBM per device.

v0:
```python
import jax
import jax.numpy as jnp
from jax import lax
from jax.sharding import PartitionSpec as P

HIGH = lax.Precision.HIGHEST


def from_partner(value, axis, bit):
    return lax.ppermute(value, axis, [(i, i ^ 1 << bit) for i in range(lax.axis_size(axis))])


def block_diagonal(blocks):
    block_count = blocks.shape[0]
    block_side = blocks.shape[1]
    eye_table = jnp.eye(block_count, dtype=blocks.dtype)
    spread_out = blocks[:, :, None, :] * eye_table[:, None, :, None]
    return spread_out.reshape(block_count * block_side, block_count * block_side)


def select_blocks(panel_cols, diag_blocks, wanted, owned_mask, block_size):
    rows_total = panel_cols.shape[0]
    local_count = panel_cols.shape[1] // block_size
    taken_blocks = (
        jnp.take(panel_cols.reshape(rows_total, local_count, block_size), wanted, axis=1)
        * owned_mask[None, :, None]
    )
    taken_diag = (
        jnp.take(diag_blocks.reshape(local_count, block_size, block_size), wanted, axis=0)
        * owned_mask[:, None, None]
    )
    return (taken_blocks.reshape(rows_total, -1), taken_diag.reshape(-1, block_size))


def child_cov(parent_cov, chosen, chosen_diag, block_size):
    block_count = chosen_diag.shape[0] // block_size
    product = jnp.dot(parent_cov, chosen, precision=HIGH, preferred_element_type=jnp.float32)
    inner_part = jnp.dot(chosen.T, product, precision=HIGH, preferred_element_type=jnp.float32)
    return inner_part + block_diagonal(chosen_diag.reshape(block_count, block_size, block_size))


def marg_terms(panel_cols, cover_cols, block_size):
    rows_total = panel_cols.shape[0]
    block_count = panel_cols.shape[1] // block_size
    terms = jnp.einsum(
        "sai,saj->aij",
        panel_cols.reshape(rows_total, block_count, block_size),
        cover_cols.reshape(rows_total, block_count, block_size),
        precision=HIGH,
    )
    return terms.reshape(block_count * block_size, block_size)


def quad_total(pieces):
    for bit_number in range(2):
        others = from_partner((pieces[0], pieces[1], pieces[2]), "leaf", bit_number)
        pieces = (pieces[0] + others[0], pieces[1] + others[1], pieces[2] + others[2])
    return pieces


def local(
    sigma_top,
    panel_top,
    diag_top,
    panel_mid,
    diag_mid,
    pattern_mid,
    panel_low,
    diag_low,
    pattern_low,
):
    block_size = diag_top.shape[1]
    struct_rows = panel_top.shape[0]
    row_count = lax.axis_size("rows")
    leaf_index = lax.axis_index("leaf")
    rows_index = lax.axis_index("rows")
    slot_blocks = pattern_mid.shape[1]
    slot_width = slot_blocks * block_size
    quad_place = leaf_index % 4
    quad_number = leaf_index // 4
    top_local = panel_top.shape[1] // block_size
    children = 2 * quad_number + jnp.arange(2, dtype=jnp.int32)
    wanted_top = pattern_mid[children].reshape(-1)
    owned_top = (wanted_top // top_local == quad_place).astype(jnp.float32)
    chosen_top, chosen_top_diag = select_blocks(
        panel_top, diag_top, wanted_top % top_local, owned_top, block_size
    )
    padded_cov = lax.dynamic_update_slice_in_dim(
        jnp.zeros((struct_rows, struct_rows), jnp.float32),
        sigma_top,
        quad_place * sigma_top.shape[0],
        0,
    )
    share_rows = struct_rows // row_count
    diag_share = chosen_top_diag.shape[0] // row_count
    pieces = (
        lax.dynamic_slice_in_dim(padded_cov, rows_index * share_rows, share_rows, 0),
        lax.dynamic_slice_in_dim(chosen_top, rows_index * share_rows, share_rows, 0),
        lax.dynamic_slice_in_dim(chosen_top_diag, rows_index * diag_share, diag_share, 0),
    )
    pieces = quad_total(pieces)
    parent_cov, chosen_all, chosen_diag_all = (
        lax.all_gather(pieces[0], "rows", axis=0, tiled=True),
        lax.all_gather(pieces[1], "rows", axis=0, tiled=True),
        lax.all_gather(pieces[2], "rows", axis=0, tiled=True),
    )
    mid_local = panel_mid.shape[1] // block_size
    pair_number = leaf_index // 2
    pair_place = leaf_index % 2 * row_count + rows_index
    low_children = 2 * pair_number + jnp.arange(2, dtype=jnp.int32)
    wanted_mid = pattern_low[low_children].reshape(-1)
    owned_mid = (wanted_mid // mid_local == pair_place).astype(jnp.float32)
    chosen_mid, chosen_mid_diag = select_blocks(
        panel_mid, diag_mid, wanted_mid % mid_local, owned_mid, block_size
    )
    summed = lax.psum((chosen_mid, chosen_mid_diag), "rows")
    partner = from_partner((summed[0], summed[1]), "leaf", 0)
    mid_all = summed[0] + partner[0]
    mid_diag_all = summed[1] + partner[1]
    share_struct = struct_rows // row_count
    cov_rows = lax.dynamic_slice_in_dim(parent_cov, rows_index * share_struct, share_struct, 0)
    cross_top = -jnp.dot(cov_rows, panel_top, precision=HIGH, preferred_element_type=jnp.float32)
    panel_rows = lax.dynamic_slice_in_dim(panel_top, rows_index * share_struct, share_struct, 0)
    partial_value = marg_terms(panel_rows, cross_top, block_size)
    piece_rows = partial_value.shape[0] // row_count
    own_diag = lax.dynamic_slice_in_dim(diag_top, rows_index * piece_rows, piece_rows, 0)
    summed_terms = lax.psum(partial_value, "rows")
    marginal_top = own_diag - lax.dynamic_slice_in_dim(
        summed_terms, rows_index * piece_rows, piece_rows, 0
    )
    child_place = leaf_index // 2 % 2
    own_slots = lax.dynamic_slice_in_dim(chosen_all, child_place * slot_width, slot_width, 1)
    own_slot_diag = lax.dynamic_slice_in_dim(
        chosen_diag_all, child_place * slot_width, slot_width, 0
    )
    mid_cov = child_cov(parent_cov, own_slots, own_slot_diag, block_size)
    cross_mid = -jnp.dot(mid_cov, panel_mid, precision=HIGH, preferred_element_type=jnp.float32)
    marginal_mid = diag_mid - marg_terms(panel_mid, cross_mid, block_size)
    low_place = leaf_index % 2
    low_slots = lax.dynamic_slice_in_dim(mid_all, low_place * slot_width, slot_width, 1)
    low_slot_diag = lax.dynamic_slice_in_dim(mid_diag_all, low_place * slot_width, slot_width, 0)
    low_cov = child_cov(mid_cov, low_slots, low_slot_diag, block_size)
    cross_low = -jnp.dot(low_cov, panel_low, precision=HIGH, preferred_element_type=jnp.float32)
    marginal_low = diag_low - marg_terms(panel_low, cross_low, block_size)
    return (cross_top, marginal_top, cross_mid, marginal_mid, cross_low, marginal_low)


def solution(mesh):
    return jax.shard_map(
        local,
        mesh=mesh,
        in_specs=(
            P("leaf", None),
            P(None, "leaf"),
            P("leaf", None),
            P(None, ("leaf", "rows")),
            P(("leaf", "rows"), None),
            P(),
            P(None, ("leaf", "rows")),
            P(("leaf", "rows"), None),
            P(),
        ),
        out_specs=(
            P("rows", "leaf"),
            P(("leaf", "rows"), None),
            P(None, ("leaf", "rows")),
            P(("leaf", "rows"), None),
            P(None, ("leaf", "rows")),
            P(("leaf", "rows"), None),
        ),
        check_vma=False,
    )
```

profile of v0, /device:TPU:0, one launch (start us, length us, event | category | flops | bytes accessed | tf_op | source)
XLA Modules:
  0.0 711.9 jit_solution(2259707078649836408)
XLA Ops:
  8.6 3.1 collective-permute-start
  11.7 23.2 %collective-permute-done = f32[256,1024]{1,0:T(8,128)S(1)} collective-permute-done((f32[256,1024]{1,0:T(8,128)S(1)}, f32[256,1024]{1,0:T(8,128)S(1)}, u32[]{:S(2)}, u32[]{:S(2)}) %collective-permute-start) | collective-permute-done | bytes 1048608 | tf_op jit(solution)/shard_map/ppermute | solution.py:10
  35.0 1.9 collective-permute-start.1
  36.9 22.5 %collective-permute-done.1 = f32[256,1024]{1,0:T(8,128)S(1)} collective-permute-done((f32[256,1024]{1,0:T(8,128)S(1)}, f32[256,1024]{1,0:T(8,128)S(1)}, u32[]{:S(2)}, u32[]{:S(2)}) %collective-permute-start.1) | collective-permute-done | bytes 1048608 | tf_op jit(solution)/shard_map/ppermute | solution.py:10
  61.5 2.3 copy.42
  63.8 2.4 copy.45
  66.2 5.1 gather_fusion.4
  71.3 9.2 %copy.46 = f32[1024,8,256]{0,2,1:T(8,128)} copy(f32[1024,8,256]{2,0,1:T(8,128)} %bitcast.66) | data formatting | bytes 16777216 | tf_op jit(solution)/shard_map/jit(_take)/gather | solution.py:25
  82.4 1.6 copy.36
  84.7 1.8 fusion.7
  86.5 5.9 fusion
  92.4 3.9 all-gather.4.cloned.1.call-done
  96.4 7.9 %convolution_negate_fusion.1 = f32[256,1536]{1,0:T(8,128)S(1)} fusion(f32[1024,1536]{1,0:T(8,128)} %param.10, f32[1024,1024]{1,0:T(8,128)} %all-gather.4.cloned.1.call-done, s32[]{:T(128)S(6)} %select_n.181), kind=kOutput, calls=%fused_computation.15 | convolution fusion | flops 4832231424 | bytes 8912900 | tf_op jit(solution)/shard_map/dot_general | solution.py:122
  104.3 1.7 copy.37
  105.9 4.2 fusion.25
  110.5 6.6 copy.39
  117.8 6.6 copy.40
  124.4 7.1 %gather_fusion.1 = f32[8,1024,256]{2,1,0:T(8,128)} fusion(f32[1024,6,256]{2,0,1:T(8,128)} %copy.40, s32[1024]{0:T(1024)S(1)} %pad_clamp_fusion.2), kind=kCustom, calls=%fused_computation.1 | custom fusion | bytes 16777248 | tf_op jit(solution)/shard_map/jit(_take)/gather | solution.py:25
  131.5 9.2 %copy.41 = f32[1024,8,256]{0,2,1:T(8,128)} copy(f32[1024,8,256]{2,0,1:T(8,128)} %bitcast.67) | data formatting | bytes 16777216 | tf_op jit(solution)/shard_map/jit(_take)/gather | solution.py:25
  141.1 2.9 fusion.6
  144.0 1.7 collective-permute-start.2
  145.8 2.1 gather_fusion.2
  148.6 54.6 %collective-permute-done.4 = f32[512,256]{1,0:T(8,128)S(1)} collective-permute-done((f32[512,256]{1,0:T(8,128)S(1)}, f32[512,256]{1,0:T(8,128)S(1)}, u32[]{:S(2)}, u32[]{:S(2)}) %collective-permute-start.4) | collective-permute-done | bytes 524320 | tf_op jit(solution)/shard_map/ppermute | solution.py:10
  203.4 1.7 collective-permute-start.5
  205.1 11.6 %collective-permute-done.5 = f32[512,256]{1,0:T(8,128)S(1)} collective-permute-done((f32[512,256]{1,0:T(8,128)S(1)}, f32[512,256]{1,0:T(8,128)S(1)}, u32[]{:S(2)}, u32[]{:S(2)}) %collective-permute-start.5) | collective-permute-done | bytes 524320 | tf_op jit(solution)/shard_map/ppermute | solution.py:10
  217.7 2.6 fusion.42
  220.3 1.7 collective-permute-start.3
  221.9 44.5 %collective-permute-done.3 = f32[256,2048]{0,1:T(8,128)S(1)} collective-permute-done((f32[256,2048]{0,1:T(8,128)S(1)}, f32[256,2048]{0,1:T(8,128)S(1)}, u32[]{:S(2)}, u32[]{:S(2)}) %collective-permute-start.3) | collective-permute-done | bytes 2097184 | tf_op jit(solution)/shard_map/ppermute | solution.py:10
  266.4 1.6 add.220
  268.1 54.4 %all-reduce.3.cloned.1.call-done = (f32[1536,256]{1,0:T(8,128)}, f32[1024,2048]{0,1:T(8,128)}, f32[2048,256]{1,0:T(8,128)}) async-done(((f32[1536,256]{1,0:T(8,128)}, f32[1024,2048]{0,1:T(8,128)}, f32[2048,256]{1,0:T(8,128)}), (f32[1536,256]{1,0:T(8,128)}, f32[1024,2048]{0,1:T(8,128)}, f32[2048,256]{1,0:T(8,128)})) %all-reduce.3.cloned.1.call-update) | async-done | bytes 12058640 | tf_op jit(solution)/shard_map/psum | solution.py:127
  324.5 6.7 copy.48
  331.2 16.3 %all-gather.8.cloned.1.call-done = f32[2048,256]{1,0:T(8,128)} async-done(((f32[512,256]{1,0:T(8,128)}), f32[2048,256]{1,0:T(8,128)}) %all-gather.8.cloned.1.call-update) | async-done | bytes 2097168 | tf_op jit(solution)/shard_map/all_gather | solution.py:105
  348.8 1.9 dynamic-slice_subtract_fusion
  350.7 198.7 %collective-permute-done.7 = f32[2048,256]{1,0:T(8,128)} collective-permute-done((f32[2048,256]{1,0:T(8,128)}, f32[2048,256]{1,0:T(8,128)}, u32[]{:S(2)}, u32[]{:S(2)}) %collective-permute-start.7) | collective-permute-done | bytes 2097184 | tf_op jit(solution)/shard_map/ppermute | solution.py:10
  550.9 1.6 broadcast_multiply_fusion
  552.5 3.0 copy.55
  555.5 3.0 copy.57
  558.5 25.9 %fusion.4 = f32[1024,1024]{1,0:T(8,128)S(1)} fusion(f32[1024,1024]{1,0:T(8,128)} %all-gather.4.cloned.1.call-done, f32[1024,2048]{0,1:T(8,128)} %all-gather.6.cloned.1.call-done, s32[]{:T(128)S(6)} %select_n.193), kind=kOutput, calls=%fused_computation.13 | convolution fusion | flops 12884901888 | bytes 12582916 | tf_op jit(solution)/shard_map/dot_general | solution.py:37
  584.4 14.0 %fusion.8 = f32[1024,1024]{1,0:T(8,128)S(1)} fusion(f32[1024,1024]{1,0:T(8,128)S(1)} %bitcast.75, f32[1024,1024]{1,0:T(8,128)S(1)} %fusion.4, f32[1024,2048]{0,1:T(8,128)S(1)} %copy-done.13, s32[]{:T(128)S(6)} %select_n.193), kind=kOutput, calls=%fused_computation.22 | convolution fusion | flops 12885950464 | bytes 16777220 | tf_op jit(solution)/shard_map/dot_general | solution.py:38
  598.4 2.0 copy-done.3
  600.4 12.4 %convolution_negate_fusion.2 = f32[1024,768]{0,1:T(8,128)} fusion(f32[1024,1024]{1,0:T(8,128)S(1)} %fusion.8, f32[1024,768]{1,0:T(8,128)S(1)} %copy-done.12), kind=kOutput, calls=%fused_computation.23 | convolution fusion | flops 9664462848 | bytes 10485760 | tf_op jit(solution)/shard_map/dot_general | solution.py:137
  612.8 4.1 copy.50
  616.9 5.3 fusion.26
  623.3 17.4 %fusion.11 = f32[1024,1024]{1,0:T(8,128)S(1)} fusion(f32[1024,1024]{1,0:T(8,128)S(1)} %copy-done.4, f32[1024,2048]{0,1:T(8,128)} %collective-permute-done.6, s32[]{:T(128)S(6)} %select_n.204, f32[1024,2048]{0,1:T(8,128)} %get-tuple-element.25), kind=kOutput, calls=%fused_computation.25 | convolution fusion | flops 12885950464 | bytes 16777220 | tf_op jit(solution)/shard_map/dot_general | solution.py:37
  640.8 16.3 %fusion.12 = f32[1024,1024]{1,0:T(8,128)S(1)} fusion(f32[1024,1024]{1,0:T(8,128)S(1)} %fusion.11, f32[1024,2048]{0,1:T(8,128)} %collective-permute-done.6, s32[]{:T(128)S(6)} %select_n.204, f32[1024,2048]{0,1:T(8,128)S(1)} %bitcast.81), kind=kOutput, calls=%fused_computation.26 | convolution fusion | flops 12885950464 | bytes 16777220 | tf_op jit(solution)/shard_map/dot_general | solution.py:38
  657.1 22.3 %convolution_negate_fusion = f32[1024,1536]{1,0:T(8,128)} fusion(f32[1024,1536]{1,0:T(8,128)S(1)} %bitcast.83, f32[1024,1024]{1,0:T(8,128)S(1)} %fusion.12, f32[1024,1024]{1,0:T(8,128)S(1)} %bitcast.89), kind=kOutput, calls=%fused_computation.8 | convolution fusion | flops 19329974272 | bytes 20971520 | tf_op jit(solution)/shard_map/dot_general | solution.py:143
  679.4 6.6 copy.47
  686.0 17.6 %fusion.27 = f32[6,256,256]{1,2,0:T(8,128)S(1)} fusion(f32[1024,6,256]{0,2,1:T(8,128)} %bitcast.72, f32[1024,6,256]{0,2,1:T(8,128)} %bitcast.70), kind=kOutput, calls=%fused_computation.78 | convolution fusion | flops 4831838208 | bytes 14155776 | tf_op jit(solution)/shard_map/sai,saj->aij/dot_general | solution.py:45
  (108 shorter events, 16.7 us)
Async XLA Ops:
  7.2 109.9 %copy-start = (s32[4,4]{1,0:T(4,128)S(1)}, s32[4,4]{1,0:T(4,128)}, u32[]{:S(2)}) copy-start(s32[4,4]{1,0:T(4,128)} %param.14) | copy-start | bytes 196
  7.2 1.2 copy-start.15
  7.2 89.2 %all-gather.4.cloned.1.call-start = ((), (), s32[]{:S(2)}) async-start(), calls=%async_computation | async-start | bytes 5242880 | tf_op jit(solution)/shard_map/all_gather | solution.py:103
  8.6 52.0 %copy-start.17 = (s32[8,4]{0,1:T(4,128)S(1)}, s32[8,4]{0,1:T(4,128)}, u32[]{:S(2)}) copy-start(s32[8,4]{0,1:T(4,128)} %param.17) | copy-start | bytes 388
  8.6 52.9 %copy-start.11 = (f32[1024,768]{1,0:T(8,128)S(1)}, f32[1024,768]{1,0:T(8,128)}, u32[]{:S(2)}) copy-start(f32[1024,768]{1,0:T(8,128)} %param.12) | copy-start | bytes 9437188
  8.6 26.2 %collective-permute-start = (f32[256,1024]{1,0:T(8,128)S(1)}, f32[256,1024]{1,0:T(8,128)S(1)}, u32[]{:S(2)}, u32[]{:S(2)}) collective-permute-start(f32[256,1024]{1,0:T(8,128)S(1)} %constant_dynamic-slice_fusion.2), channel_id=1, source_target_pairs={{0,4},{4,0},{8,12},{12,8},{16,20},{20,16},{24,28},{28,24},{1,5},{5... | collective-permute-start | bytes 3145736 | tf_op jit(solution)/shard_map/ppermute | solution.py:10
  35.0 24.4 %collective-permute-start.1 = (f32[256,1024]{1,0:T(8,128)S(1)}, f32[256,1024]{1,0:T(8,128)S(1)}, u32[]{:S(2)}, u32[]{:S(2)}) collective-permute-start(f32[256,1024]{1,0:T(8,128)S(1)} %fusion.44), channel_id=1, source_target_pairs={{0,8},{4,12},{8,0},{12,4},{16,24},{20,28},{24,16},{28,20},{1,9},{5... | collective-permute-start | bytes 3145736 | tf_op jit(solution)/shard_map/ppermute | solution.py:10
  60.6 261.9 %all-reduce.3.cloned.1.call-start = ((), (), s32[]{:S(2)}) async-start(), calls=%async_computation.3 | async-start | bytes 24117248 | tf_op jit(solution)/shard_map/psum | solution.py:127
  80.5 3.5 copy-start.6
  92.4 13.5 %copy-start.9 = (f32[256,1536]{0,1:T(8,128)S(1)}, f32[256,1536]{0,1:T(8,128)}, u32[]{:S(2)}) copy-start(f32[256,1536]{0,1:T(8,128)} %copy.36) | copy-start | bytes 4718596
  104.3 5.9 copy-start.8
  110.2 237.4 %all-gather.8.cloned.1.call-start = ((), (), s32[]{:S(2)}) async-start(), calls=%async_computation.2 | async-start | bytes 2621440 | tf_op jit(solution)/shard_map/all_gather | solution.py:105
  144.0 73.7 %collective-permute-start.2 = (f32[256,2048]{0,1:T(8,128)}, f32[256,2048]{0,1:T(8,128)}, u32[]{:S(2)}, u32[]{:S(2)}) collective-permute-start(f32[256,2048]{0,1:T(8,128)} %fusion.6), channel_id=1, source_target_pairs={{0,4},{4,0},{8,12},{12,8},{16,20},{20,16},{24,28},{28,24},{1,5},{5... | collective-permute-start | bytes 6291464 | tf_op jit(solution)/shard_map/ppermute | solution.py:10
  148.1 55.0 %collective-permute-start.4 = (f32[512,256]{1,0:T(8,128)S(1)}, f32[512,256]{1,0:T(8,128)S(1)}, u32[]{:S(2)}, u32[]{:S(2)}) collective-permute-start(f32[512,256]{1,0:T(8,128)S(1)} %fusion.14), channel_id=1, source_target_pairs={{0,4},{4,0},{8,12},{12,8},{16,20},{20,16},{24,28},{28,24},{1,5},{5... | collective-permute-start | bytes 1572872 | tf_op jit(solution)/shard_map/ppermute | solution.py:10
  203.4 13.3 %collective-permute-start.5 = (f32[512,256]{1,0:T(8,128)S(1)}, f32[512,256]{1,0:T(8,128)S(1)}, u32[]{:S(2)}, u32[]{:S(2)}) collective-permute-start(f32[512,256]{1,0:T(8,128)S(1)} %fusion.43), channel_id=1, source_target_pairs={{0,8},{4,12},{8,0},{12,4},{16,24},{20,28},{24,16},{28,20},{1,9},{5... | collective-permute-start | bytes 1572872 | tf_op jit(solution)/shard_map/ppermute | solution.py:10
  217.6 340.9 %all-gather.6.cloned.1.call-start = ((), (), s32[]{:S(2)}) async-start(), calls=%async_computation.1 | async-start | bytes 10485760 | tf_op jit(solution)/shard_map/all_gather | solution.py:104
  220.3 46.2 %collective-permute-start.3 = (f32[256,2048]{0,1:T(8,128)S(1)}, f32[256,2048]{0,1:T(8,128)S(1)}, u32[]{:S(2)}, u32[]{:S(2)}) collective-permute-start(f32[256,2048]{0,1:T(8,128)S(1)} %fusion.42), channel_id=1, source_target_pairs={{0,8},{4,12},{8,0},{12,4},{16,24},{20,28},{24,16},{28,20},{1,9},{5... | collective-permute-start | bytes 6291464 | tf_op jit(solution)/shard_map/ppermute | solution.py:10
  322.5 300.8 %collective-permute-start.6 = (f32[1024,2048]{0,1:T(8,128)}, f32[1024,2048]{0,1:T(8,128)}, u32[]{:S(2)}, u32[]{:S(2)}) collective-permute-start(f32[1024,2048]{0,1:T(8,128)} %get-tuple-element.25), channel_id=1, source_target_pairs={{0,4},{4,0},{8,12},{12,8},{16,20},{20,16},{24,28},{28,24},{1,5},{5... | collective-permute-start | bytes 25165832 | tf_op jit(solution)/shard_map/ppermute | solution.py:10
  324.0 225.5 %collective-permute-start.7 = (f32[2048,256]{1,0:T(8,128)}, f32[2048,256]{1,0:T(8,128)}, u32[]{:S(2)}, u32[]{:S(2)}) collective-permute-start(f32[2048,256]{1,0:T(8,128)} %get-tuple-element.26), channel_id=1, source_target_pairs={{0,4},{4,0},{8,12},{12,8},{16,20},{20,16},{24,28},{28,24},{1,5},{5... | collective-permute-start | bytes 6291464 | tf_op jit(solution)/shard_map/ppermute | solution.py:10
  324.5 225.0 %copy-start.16 = (f32[2048,256]{1,0:T(8,128)S(1)}, f32[2048,256]{1,0:T(8,128)}, u32[]{:S(2)}) copy-start(f32[2048,256]{1,0:T(8,128)} %get-tuple-element.26) | copy-start | bytes 6291460
  558.5 25.9 %copy-start.5 = (f32[128,8,4,256]{3,1,2,0:T(8,128)S(1)}, f32[128,8,4,256]{3,1,2,0:T(8,128)}, u32[]{:S(2)}) copy-start(f32[128,8,4,256]{3,1,2,0:T(8,128)} %copy.55) | copy-start | bytes 12582916
  558.5 25.9 %copy-start.13 = (f32[1024,2048]{0,1:T(8,128)S(1)}, f32[1024,2048]{0,1:T(8,128)}, u32[]{:S(2)}) copy-start(f32[1024,2048]{0,1:T(8,128)} %all-gather.6.cloned.1.call-done) | copy-start | bytes 25165828
  584.4 16.0 %copy-start.12 = (f32[1024,768]{1,0:T(8,128)S(1)}, f32[1024,768]{1,0:T(8,128)}, u32[]{:S(2)}) copy-start(f32[1024,768]{1,0:T(8,128)} %param.12) | copy-start | bytes 9437188
  598.4 2.0 copy-start.3
  612.8 4.1 copy-start.2
  616.9 5.4 copy-start.7
  616.9 6.4 copy-start.4
  622.2 18.5 %slice-start = ((s8[8388608]{0:T(1024)(128)(4,1)}), s8[4194304]{0:T(1024)(128)(4,1)S(1)}, s32[]{:S(2)}) async-start(s8[8388608]{0:T(1024)(128)(4,1)} %bitcast.80), calls=%async_computation.4 | async-start | bytes 8388608
  623.3 17.4 %slice-start.1 = ((s8[8388608]{0:T(1024)(128)(4,1)}), s8[4194304]{0:T(1024)(128)(4,1)S(1)}, s32[]{:S(2)}) async-start(s8[8388608]{0:T(1024)(128)(4,1)} %bitcast.80), calls=%async_computation.5 | async-start | bytes 8388608
  623.3 33.8 %slice-start.2 = ((s8[6291456]{0:T(1024)(128)(4,1)}), s8[4194304]{0:T(1024)(128)(4,1)S(1)}, s32[]{:S(2)}) async-start(s8[6291456]{0:T(1024)(128)(4,1)} %bitcast.82), calls=%async_computation.6 | async-start | bytes 8388608
  640.7 16.3 %slice-start.3 = ((s8[6291456]{0:T(1024)(128)(4,1)}), s8[2097152]{0:T(1024)(128)(4,1)S(1)}, s32[]{:S(2)}) async-start(s8[6291456]{0:T(1024)(128)(4,1)} %bitcast.82), calls=%async_computation.7 | async-start | bytes 4194304
  640.8 16.3 %copy-start.10 = (f32[128,8,4,256]{3,1,2,0:T(8,128)S(1)}, f32[128,8,4,256]{3,1,2,0:T(8,128)}, u32[]{:S(2)}) copy-start(f32[128,8,4,256]{3,1,2,0:T(8,128)} %copy.57) | copy-start | bytes 12582916
  686.0 17.6 %copy-start.14 = (f32[1536,256]{1,0:T(8,128)S(1)}, f32[1536,256]{1,0:T(8,128)}, u32[]{:S(2)}) copy-start(f32[1536,256]{1,0:T(8,128)} %param.16) | copy-start | bytes 4718596
  686.0 18.9 %copy-start.1 = (s32[4,4]{1,0:T(4,128)S(1)}, s32[4,4]{1,0:T(4,128)}, u32[]{:S(2)}) copy-start(s32[4,4]{1,0:T(4,128)} %param.14) | copy-start | bytes 196
Sparse Core Ops, SparseCore 0:
  60.7 35.6 all-gather.3
  110.3 212.1 all-reduce.2
  324.6 22.8 all-gather.7
  348.9 58.2 all-gather.5
where the time goes:
time: 720 us; the launch traced here: 712 us
  waiting for transfers between devices  430 us (60%)
  matrix products  143 us (20%)
  local copies, waits for them, and re-layouts  86.5 us (12%)
  other arithmetic  24.8 us (3%)
  between operations  14.7 us (2%)
  starting transfers between devices  12.9 us (2%)
    ppermute x8, waiting for transfers between devices, from_partner(): lax.ppermute(value, axis, [(i, i ^ 1 << bit) for i in range(lax.axis_size...  355 us
    psum x1, waiting for transfers between devices, local(): summed_terms = lax.psum(partial_value, 'rows')  54.4 us
    dot_general x2, matrix products, child_cov(): jnp.dot(parent_cov, chosen, precision=HIGH, preferred_element_type=jnp.fl...  43.3 us
    gather x4, local copies, waits for them, and re-layouts, select_blocks(): jnp.take(panel_cols.reshape(rows_total, local_count, block_size), wanted,...  30.7 us
    dot_general x2, matrix products, child_cov(): jnp.dot(chosen.T, product, precision=HIGH, preferred_element_type=jnp.flo...  30.3 us
    unnamed x55, local copies, waits for them, and re-layouts  28.7 us
    dot_general x3, matrix products, marg_terms(): jnp.einsum('sai,saj->aij', panel_cols.reshape(rows_total, block_count, bl...  27.1 us
    dot_general x1, matrix products, local(): jnp.dot(low_cov, panel_low, precision=HIGH, preferred_element_type=jnp.fl...  22.3 us
  transfers between devices with their start and end apart: 12, of which 9 were waited for; matrix products, arithmetic and copies ran while one was open for 22% of the time, Pallas kernels for 0%

commit v1 on v0

--- a/solution.py
+++ b/solution.py
@@ -124,7 +124,8 @@
     partial_value = marg_terms(panel_rows, cross_top, block_size)
     piece_rows = partial_value.shape[0] // row_count
     own_diag = lax.dynamic_slice_in_dim(diag_top, rows_index * piece_rows, piece_rows, 0)
-    summed_terms = lax.psum(partial_value, "rows")
+    parts = lax.all_gather(partial_value, "rows", axis=0, tiled=False)
+    summed_terms = parts.sum(axis=0)
     marginal_top = own_diag - lax.dynamic_slice_in_dim(
         summed_terms, rows_index * piece_rows, piece_rows, 0
     )

time: 720 us -> 636 us (0.88)
  waiting for transfers between devices: 430 us -> 352 us
    psum x1, waiting for transfers between devices: 54.4 us -> 0.02 us  [local(): summed = lax.psum((chosen_mid, chosen_mid_diag), 'rows')]
    ppermute x8, waiting for transfers between devices: 355 us -> 333 us  [from_partner(): lax.ppermute(value, axis, [(i, i ^ 1 << bit) for i in range(lax.axis_size...]
    all_gather x1, waiting for transfers between devices: 16.3 us -> 2.39 us  [local(): lax.all_gather(pieces[2], 'rows', axis=0, tiled=True)]
    all_gather x1, waiting for transfers between devices: 3.92 us -> 16.1 us  [local(): lax.all_gather(pieces[0], 'rows', axis=0, tiled=True)]
    dot_general x2, matrix products: 43.3 us -> 35.1 us  [child_cov(): jnp.dot(parent_cov, chosen, precision=HIGH, preferred_element_type=jnp.fl...]
    unnamed x55 -> x45, local copies, waits for them, and re-layouts: 28.7 us -> 28.2 us
  transfers between devices with their start and end apart: 12 -> 13, of which waited for: 9 -> 8; matrix products, arithmetic and copies ran while one was open for 22% -> 34% of each run, Pallas kernels for 0% -> 0%
where the time goes in v1:
time: 636 us; the launch traced here: 629 us
  waiting for transfers between devices  352 us (55%)
  matrix products  138 us (22%)
  local copies, waits for them, and re-layouts  84.5 us (13%)
  other arithmetic  28 us (4%)
  between operations  14.4 us (2%)
  starting transfers between devices  12.1 us (2%)
    ppermute x8, waiting for transfers between devices, from_partner(): lax.ppermute(value, axis, [(i, i ^ 1 << bit) for i in range(lax.axis_size...  333 us
    dot_general x2, matrix products, child_cov(): jnp.dot(parent_cov, chosen, precision=HIGH, preferred_element_type=jnp.fl...  35.1 us
    dot_general x2, matrix products, child_cov(): jnp.dot(chosen.T, product, precision=HIGH, preferred_element_type=jnp.flo...  32.7 us
    gather x4, local copies, waits for them, and re-layouts, select_blocks(): jnp.take(panel_cols.reshape(rows_total, local_count, block_size), wanted,...  30 us
    unnamed x45, local copies, waits for them, and re-layouts  28.2 us
    dot_general x3, matrix products, marg_terms(): jnp.einsum('sai,saj->aij', panel_cols.reshape(rows_total, block_count, bl...  27 us
    dot_general x1, matrix products, local(): jnp.dot(low_cov, panel_low, precision=HIGH, preferred_element_type=jnp.fl...  22.1 us
    all_gather x1, waiting for transfers between devices, local(): lax.all_gather(pieces[0], 'rows', axis=0, tiled=True)  16.1 us
  transfers between devices with their start and end apart: 13, of which 8 were waited for; matrix products, arithmetic and copies ran while one was open for 34% of the time, Pallas kernels for 0%

profile of v1, /device:TPU:0, one launch (start us, length us, event | category | flops | bytes accessed | tf_op | source)
XLA Modules:
  0.0 629.1 jit_solution(7430282009033751968)
XLA Ops:
  8.8 3.5 copy.57
  12.3 2.4 copy.60
  14.7 4.3 gather_fusion.4
  19.1 9.2 %copy.61 = f32[1024,8,256]{0,2,1:T(8,128)} copy(f32[1024,8,256]{2,0,1:T(8,128)} %bitcast.66) | data formatting | bytes 16777216 | tf_op jit(solution)/shard_map/jit(_take)/gather | solution.py:25
  29.3 5.9 fusion
  35.2 1.8 fusion.7
  38.4 3.1 collective-permute-start
  41.5 23.2 %collective-permute-done = f32[256,1024]{1,0:T(8,128)S(1)} collective-permute-done((f32[256,1024]{1,0:T(8,128)S(1)}, f32[256,1024]{1,0:T(8,128)S(1)}, u32[]{:S(2)}, u32[]{:S(2)}) %collective-permute-start) | collective-permute-done | bytes 1048608 | tf_op jit(solution)/shard_map/ppermute | solution.py:10
  64.8 1.9 collective-permute-start.1
  66.7 22.6 %collective-permute-done.1 = f32[256,1024]{1,0:T(8,128)S(1)} collective-permute-done((f32[256,1024]{1,0:T(8,128)S(1)}, f32[256,1024]{1,0:T(8,128)S(1)}, u32[]{:S(2)}, u32[]{:S(2)}) %collective-permute-start.1) | collective-permute-done | bytes 1048608 | tf_op jit(solution)/shard_map/ppermute | solution.py:10
  91.3 6.6 %copy.54 = f32[1024,1536]{0,1:T(8,128)} copy(f32[1024,1536]{1,0:T(8,128)} %param.10) | data formatting | bytes 12582912 | tf_op args[1]
  97.9 6.6 %copy.55 = f32[1024,6,256]{2,0,1:T(8,128)} copy(f32[1024,6,256]{0,2,1:T(8,128)} %bitcast.72) | data formatting | bytes 12582912 | tf_op jit(solution)/shard_map/reshape | solution.py:25
  104.6 7.2 %gather_fusion.1 = f32[8,1024,256]{2,1,0:T(8,128)} fusion(f32[1024,6,256]{2,0,1:T(8,128)} %copy.55, s32[1024]{0:T(1024)S(1)} %pad_clamp_fusion.2), kind=kCustom, calls=%fused_computation.1 | custom fusion | bytes 16777248 | tf_op jit(solution)/shard_map/jit(_take)/gather | solution.py:25
  111.8 9.2 %copy.56 = f32[1024,8,256]{0,2,1:T(8,128)} copy(f32[1024,8,256]{2,0,1:T(8,128)} %bitcast.67) | data formatting | bytes 16777216 | tf_op jit(solution)/shard_map/jit(_take)/gather | solution.py:25
  121.4 2.9 fusion.6
  124.3 1.4 collective-permute-start.2
  125.8 2.1 gather_fusion.2
  128.8 53.2 %collective-permute-done.4 = f32[512,256]{1,0:T(8,128)S(1)} collective-permute-done((f32[512,256]{1,0:T(8,128)S(1)}, f32[512,256]{1,0:T(8,128)S(1)}, u32[]{:S(2)}, u32[]{:S(2)}) %collective-permute-start.4) | collective-permute-done | bytes 524320 | tf_op jit(solution)/shard_map/ppermute | solution.py:10
  183.5 10.7 %collective-permute-done.5 = f32[512,256]{1,0:T(8,128)S(1)} collective-permute-done((f32[512,256]{1,0:T(8,128)S(1)}, f32[512,256]{1,0:T(8,128)S(1)}, u32[]{:S(2)}, u32[]{:S(2)}) %collective-permute-start.5) | collective-permute-done | bytes 524320 | tf_op jit(solution)/shard_map/ppermute | solution.py:10
  195.2 2.6 fusion.42
  198.8 43.9 %collective-permute-done.3 = f32[256,2048]{0,1:T(8,128)S(1)} collective-permute-done((f32[256,2048]{0,1:T(8,128)S(1)}, f32[256,2048]{0,1:T(8,128)S(1)}, u32[]{:S(2)}, u32[]{:S(2)}) %collective-permute-start.3) | collective-permute-done | bytes 2097184 | tf_op jit(solution)/shard_map/ppermute | solution.py:10
  242.7 1.6 add.218
  245.4 1.5 constant_dynamic-slice_fusion.1
  247.4 16.1 %all-gather.5.cloned.1.call-done = f32[1024,1024]{1,0:T(8,128)} async-done(((f32[256,1024]{1,0:T(8,128)}), f32[1024,1024]{1,0:T(8,128)}) %all-gather.5.cloned.1.call-update) | async-done | bytes 4194320 | tf_op jit(solution)/shard_map/all_gather | solution.py:103
  263.5 7.9 %convolution_negate_fusion.1 = f32[256,1536]{1,0:T(8,128)S(1)} fusion(f32[1024,1536]{1,0:T(8,128)} %param.10, f32[1024,1024]{1,0:T(8,128)} %all-gather.5.cloned.1.call-done, s32[]{:T(128)S(6)} %select_n.181), kind=kOutput, calls=%fused_computation.15 | convolution fusion | flops 4832231424 | bytes 8912900 | tf_op jit(solution)/shard_map/dot_general | solution.py:122
  271.4 1.7 copy.52
  273.1 4.4 fusion.25
  277.5 1.6 collective-permute-start.7
  279.1 6.7 %copy.63 = f32[1024,1536]{0,1:T(8,128)} copy(f32[1024,1536]{1,0:T(8,128)} %param.15) | data formatting | bytes 12582912 | tf_op args[6]
  285.8 2.4 all-gather.11.cloned.1.call-done
  289.5 179.4 %collective-permute-done.7 = f32[2048,256]{1,0:T(8,128)} collective-permute-done((f32[2048,256]{1,0:T(8,128)}, f32[2048,256]{1,0:T(8,128)}, u32[]{:S(2)}, u32[]{:S(2)}) %collective-permute-start.7) | collective-permute-done | bytes 2097184 | tf_op jit(solution)/shard_map/ppermute | solution.py:10
  468.9 1.4 dynamic-slice_add_fusion.3
  470.3 1.6 broadcast_multiply_fusion
  471.9 3.0 copy.70
  474.9 3.0 copy.72
  478.0 17.3 %fusion.4 = f32[1024,1024]{1,0:T(8,128)S(1)} fusion(f32[1024,1024]{1,0:T(8,128)} %all-gather.5.cloned.1.call-done, f32[1024,2048]{0,1:T(8,128)} %all-gather.9.cloned.1.call-done, s32[]{:T(128)S(6)} %select_n.193), kind=kOutput, calls=%fused_computation.13 | convolution fusion | flops 12884901888 | bytes 12582916 | tf_op jit(solution)/shard_map/dot_general | solution.py:37
  495.3 16.1 %fusion.8 = f32[1024,1024]{1,0:T(8,128)S(1)} fusion(f32[1024,1024]{1,0:T(8,128)S(1)} %bitcast.75, f32[1024,1024]{1,0:T(8,128)S(1)} %fusion.4, f32[1024,2048]{0,1:T(8,128)} %all-gather.9.cloned.1.call-done, s32[]{:T(128)S(6)} %select_n.193), kind=kOutput, calls=%fused_computation.22 | convolution fusion | flops 12885950464 | bytes 16777220 | tf_op jit(solution)/shard_map/dot_general | solution.py:38
  511.5 17.8 %fusion.11 = f32[1024,1024]{1,0:T(8,128)S(1)} fusion(f32[1024,1024]{1,0:T(8,128)S(1)} %fusion.8, f32[1024,2048]{0,1:T(8,128)} %collective-permute-done.6, s32[]{:T(128)S(6)} %select_n.204, f32[1024,2048]{0,1:T(8,128)S(1)} %bitcast.81), kind=kOutput, calls=%fused_computation.25 | convolution fusion | flops 12885950464 | bytes 16777220 | tf_op jit(solution)/shard_map/dot_general | solution.py:37
  529.3 16.5 %fusion.12 = f32[1024,1024]{1,0:T(8,128)S(1)} fusion(f32[1024,1024]{1,0:T(8,128)S(1)} %fusion.11, f32[1024,2048]{0,1:T(8,128)} %collective-permute-done.6, s32[]{:T(128)S(6)} %select_n.204, f32[1024,2048]{0,1:T(8,128)S(1)} %bitcast.81), kind=kOutput, calls=%fused_computation.26 | convolution fusion | flops 12885950464 | bytes 16777220 | tf_op jit(solution)/shard_map/dot_general | solution.py:38
  545.9 22.1 %convolution_negate_fusion = f32[1024,1536]{1,0:T(8,128)} fusion(f32[1024,1536]{1,0:T(8,128)S(1)} %bitcast.83, f32[1024,1024]{1,0:T(8,128)S(1)} %fusion.12, f32[1024,1024]{1,0:T(8,128)S(1)} %bitcast.89), kind=kOutput, calls=%fused_computation.8 | convolution fusion | flops 19329974272 | bytes 20971520 | tf_op jit(solution)/shard_map/dot_general | solution.py:144
  568.0 6.7 %copy.62 = f32[1024,1536]{0,1:T(8,128)} copy(f32[1024,1536]{1,0:T(8,128)} %convolution_negate_fusion) | data formatting | bytes 12582912 | tf_op jit(solution)/shard_map/neg | solution.py:144
  574.7 13.6 %convolution_negate_fusion.2 = f32[1024,768]{0,1:T(8,128)} fusion(f32[1024,1024]{1,0:T(8,128)} %copy-done.3, f32[1024,768]{1,0:T(8,128)S(1)} %copy-done.9), kind=kOutput, calls=%fused_computation.23 | convolution fusion | flops 9664462848 | bytes 10485760 | tf_op jit(solution)/shard_map/dot_general | solution.py:138
  588.4 3.7 copy.65
  592.1 5.2 fusion.26
  598.3 17.4 %fusion.27 = f32[6,256,256]{1,2,0:T(8,128)S(1)} fusion(f32[1024,6,256]{0,2,1:T(8,128)} %bitcast.71, f32[1024,6,256]{0,2,1:T(8,128)} %bitcast.70), kind=kOutput, calls=%fused_computation.78 | convolution fusion | flops 4831838208 | bytes 14155776 | tf_op jit(solution)/shard_map/sai,saj->aij/dot_general | solution.py:45
  615.8 1.3 bitcast_subtract_fusion
  617.1 3.5 reduce_sum.9
  620.6 1.8 dynamic-slice_subtract_fusion
  (102 shorter events, 14.7 us)
Async XLA Ops:
  7.2 83.4 %copy-start = (s32[4,4]{1,0:T(4,128)S(1)}, s32[4,4]{1,0:T(4,128)}, u32[]{:S(2)}) copy-start(s32[4,4]{1,0:T(4,128)} %param.14) | copy-start | bytes 196
  7.2 237.6 %all-reduce.3.cloned.1.call-start = ((), (), s32[]{:S(2)}) async-start(), calls=%async_computation.4 | async-start | bytes 20971520 | tf_op jit(solution)/shard_map/psum | solution.py:116
  19.1 9.6 %copy-start.5 = (f32[768,256]{1,0:T(8,128)S(1)}, f32[768,256]{1,0:T(8,128)}, u32[]{:S(2)}) copy-start(f32[768,256]{1,0:T(8,128)} %param.13) | copy-start | bytes 2359300
  37.0 1.2 copy-start.11
  37.0 226.4 %all-gather.5.cloned.1.call-start = ((), (), s32[]{:S(2)}) async-start(), calls=%async_computation | async-start | bytes 5242880 | tf_op jit(solution)/shard_map/all_gather | solution.py:103
  38.4 26.2 %collective-permute-start = (f32[256,1024]{1,0:T(8,128)S(1)}, f32[256,1024]{1,0:T(8,128)S(1)}, u32[]{:S(2)}, u32[]{:S(2)}) collective-permute-start(f32[256,1024]{1,0:T(8,128)S(1)} %constant_dynamic-slice_fusion.2), channel_id=1, source_target_pairs={{0,4},{4,0},{8,12},{12,8},{16,20},{20,16},{24,28},{28,24},{1,5},{5... | collective-permute-start | bytes 3145736 | tf_op jit(solution)/shard_map/ppermute | solution.py:10
  64.8 24.5 %collective-permute-start.1 = (f32[256,1024]{1,0:T(8,128)S(1)}, f32[256,1024]{1,0:T(8,128)S(1)}, u32[]{:S(2)}, u32[]{:S(2)}) collective-permute-start(f32[256,1024]{1,0:T(8,128)S(1)} %fusion.44), channel_id=1, source_target_pairs={{0,8},{4,12},{8,0},{12,4},{16,24},{20,28},{24,16},{28,20},{1,9},{5... | collective-permute-start | bytes 3145736 | tf_op jit(solution)/shard_map/ppermute | solution.py:10
  90.5 197.7 %all-gather.11.cloned.1.call-start = ((), (), s32[]{:S(2)}) async-start(), calls=%async_computation.3 | async-start | bytes 2621440 | tf_op jit(solution)/shard_map/all_gather | solution.py:105
  124.3 70.9 %collective-permute-start.2 = (f32[256,2048]{0,1:T(8,128)}, f32[256,2048]{0,1:T(8,128)}, u32[]{:S(2)}, u32[]{:S(2)}) collective-permute-start(f32[256,2048]{0,1:T(8,128)} %fusion.6), channel_id=1, source_target_pairs={{0,4},{4,0},{8,12},{12,8},{16,20},{20,16},{24,28},{28,24},{1,5},{5... | collective-permute-start | bytes 6291464 | tf_op jit(solution)/shard_map/ppermute | solution.py:10
  128.2 53.9 %collective-permute-start.4 = (f32[512,256]{1,0:T(8,128)S(1)}, f32[512,256]{1,0:T(8,128)S(1)}, u32[]{:S(2)}, u32[]{:S(2)}) collective-permute-start(f32[512,256]{1,0:T(8,128)S(1)} %fusion.14), channel_id=1, source_target_pairs={{0,4},{4,0},{8,12},{12,8},{16,20},{20,16},{24,28},{28,24},{1,5},{5... | collective-permute-start | bytes 1572872 | tf_op jit(solution)/shard_map/ppermute | solution.py:10
  182.3 12.0 %collective-permute-start.5 = (f32[512,256]{1,0:T(8,128)S(1)}, f32[512,256]{1,0:T(8,128)S(1)}, u32[]{:S(2)}, u32[]{:S(2)}) collective-permute-start(f32[512,256]{1,0:T(8,128)S(1)} %fusion.43), channel_id=1, source_target_pairs={{0,8},{4,12},{8,0},{12,4},{16,24},{20,28},{24,16},{28,20},{1,9},{5... | collective-permute-start | bytes 1572872 | tf_op jit(solution)/shard_map/ppermute | solution.py:10
  195.1 282.8 %all-gather.9.cloned.1.call-start = ((), (), s32[]{:S(2)}) async-start(), calls=%async_computation.2 | async-start | bytes 10485760 | tf_op jit(solution)/shard_map/all_gather | solution.py:104
  197.8 44.8 %collective-permute-start.3 = (f32[256,2048]{0,1:T(8,128)S(1)}, f32[256,2048]{0,1:T(8,128)S(1)}, u32[]{:S(2)}, u32[]{:S(2)}) collective-permute-start(f32[256,2048]{0,1:T(8,128)S(1)} %fusion.42), channel_id=1, source_target_pairs={{0,8},{4,12},{8,0},{12,4},{16,24},{20,28},{24,16},{28,20},{1,9},{5... | collective-permute-start | bytes 6291464 | tf_op jit(solution)/shard_map/ppermute | solution.py:10
  244.2 372.9 %all-gather.7.cloned.1.call-start = ((), (), s32[]{:S(2)}) async-start(), calls=%async_computation.1 | async-start | bytes 7864320 | tf_op jit(solution)/shard_map/all_gather | solution.py:127
  244.8 266.6 %collective-permute-start.6 = (f32[1024,2048]{0,1:T(8,128)}, f32[1024,2048]{0,1:T(8,128)}, u32[]{:S(2)}, u32[]{:S(2)}) collective-permute-start(f32[1024,2048]{0,1:T(8,128)} %get-tuple-element.30), channel_id=1, source_target_pairs={{0,4},{4,0},{8,12},{12,8},{16,20},{20,16},{24,28},{28,24},{1,5},{5... | collective-permute-start | bytes 25165832 | tf_op jit(solution)/shard_map/ppermute | solution.py:10
  271.4 6.0 copy-start.7
  277.5 191.4 %collective-permute-start.7 = (f32[2048,256]{1,0:T(8,128)}, f32[2048,256]{1,0:T(8,128)}, u32[]{:S(2)}, u32[]{:S(2)}) collective-permute-start(f32[2048,256]{1,0:T(8,128)} %get-tuple-element.31), channel_id=1, source_target_pairs={{0,4},{4,0},{8,12},{12,8},{16,20},{20,16},{24,28},{28,24},{1,5},{5... | collective-permute-start | bytes 6291464 | tf_op jit(solution)/shard_map/ppermute | solution.py:10
  279.1 189.8 %copy-start.12 = (f32[2048,256]{1,0:T(8,128)S(1)}, f32[2048,256]{1,0:T(8,128)}, u32[]{:S(2)}) copy-start(f32[2048,256]{1,0:T(8,128)} %get-tuple-element.31) | copy-start | bytes 6291460
  477.9 17.3 %copy-start.4 = (f32[128,8,4,256]{3,1,2,0:T(8,128)S(1)}, f32[128,8,4,256]{3,1,2,0:T(8,128)}, u32[]{:S(2)}) copy-start(f32[128,8,4,256]{3,1,2,0:T(8,128)} %copy.70) | copy-start | bytes 12582916
  477.9 33.5 %slice-start = ((s8[8388608]{0:T(1024)(128)(4,1)}), s8[4194304]{0:T(1024)(128)(4,1)S(1)}, s32[]{:S(2)}) async-start(s8[8388608]{0:T(1024)(128)(4,1)} %bitcast.80), calls=%async_computation.5 | async-start | bytes 8388608
  495.3 16.2 %slice-start.1 = ((s8[8388608]{0:T(1024)(128)(4,1)}), s8[4194304]{0:T(1024)(128)(4,1)S(1)}, s32[]{:S(2)}) async-start(s8[8388608]{0:T(1024)(128)(4,1)} %bitcast.80), calls=%async_computation.6 | async-start | bytes 8388608
  511.4 17.9 %copy-start.3 = (f32[1024,1024]{1,0:T(8,128)}, f32[1024,1024]{1,0:T(8,128)S(1)}, u32[]{:S(2)}) copy-start(f32[1024,1024]{1,0:T(8,128)S(1)} %fusion.8) | copy-start | bytes 12582916
  511.5 34.4 %slice-start.2 = ((s8[6291456]{0:T(1024)(128)(4,1)}), s8[4194304]{0:T(1024)(128)(4,1)S(1)}, s32[]{:S(2)}) async-start(s8[6291456]{0:T(1024)(128)(4,1)} %bitcast.82), calls=%async_computation.7 | async-start | bytes 8388608
  529.3 16.6 %slice-start.3 = ((s8[6291456]{0:T(1024)(128)(4,1)}), s8[2097152]{0:T(1024)(128)(4,1)S(1)}, s32[]{:S(2)}) async-start(s8[6291456]{0:T(1024)(128)(4,1)} %bitcast.82), calls=%async_computation.8 | async-start | bytes 4194304
  529.3 16.6 %copy-start.8 = (f32[128,8,4,256]{3,1,2,0:T(8,128)S(1)}, f32[128,8,4,256]{3,1,2,0:T(8,128)}, u32[]{:S(2)}) copy-start(f32[128,8,4,256]{3,1,2,0:T(8,128)} %copy.72) | copy-start | bytes 12582916
  568.0 6.7 %copy-start.9 = (f32[1024,768]{1,0:T(8,128)S(1)}, f32[1024,768]{1,0:T(8,128)}, u32[]{:S(2)}) copy-start(f32[1024,768]{1,0:T(8,128)} %param.12) | copy-start | bytes 9437188
  588.4 3.7 copy-start.2
  592.1 5.3 copy-start.6
  598.3 17.4 %copy-start.10 = (f32[1536,256]{1,0:T(8,128)S(1)}, f32[1536,256]{1,0:T(8,128)}, u32[]{:S(2)}) copy-start(f32[1536,256]{1,0:T(8,128)} %param.16) | copy-start | bytes 4718596
  615.8 6.6 %copy-start.1 = (s32[4,4]{1,0:T(4,128)S(1)}, s32[4,4]{1,0:T(4,128)}, u32[]{:S(2)}) copy-start(s32[4,4]{1,0:T(4,128)} %param.14) | copy-start | bytes 196
Sparse Core Ops, SparseCore 0:
  37.1 189.4 all-reduce.2
  228.8 34.6 all-gather.4
  265.6 22.5 all-gather.10
  289.6 58.2 all-gather.8
  349.3 46.3 all-gather.6
